TPU v7x, 256 devices: a whole 4x4x8 slice. The times are simulated.
256 devices in a mesh: row: 16 (over z_hi, y), col: 16 (over x, z_lo, core).
Axes of the slice: x: 4, y: 4, z: 8 (z_hi: 4, z_lo: 2; z = z_hi * 2 + z_lo), core: 2. Of those that a mesh axis runs over, the one named last changes fastest.
Arguments:
- positions: float32 [3, 32768], P(None, ('row', 'col')), may hold values from 0 to 1
- radii: float32 [32768], P(('row', 'col')), may hold values from 0.5 to 2
- right_side: float32 [32768, 256], P(('row', 'col')), may hold values from -60 to 60, as said below
Outputs:
- solution: float32 [32768, 256], P(('row', 'col'))
- residual: float32 [32768, 256], P(('row', 'col'))
Inputs may be any that keep to these rules, and one draw needn't show every extreme that they name: `right_side`: real values of varying scale.
All inputs are finite; a program needn't handle non-finite values.
Results may differ from a plain program's by a relative error of at most 0.0003.
Values sent between devices are 32-bit elements; how exact they have to be, the bound alone decides.
A program may use at most 64 MiB of HBM per device.

v0:
```python
import jax
import jax.numpy as jnp
from jax import lax
from jax.sharding import PartitionSpec as P

ITERS = 2


def kernel_product(row_points, col_points, values, kernel_scale, softening, limit):
    row_count = row_points.shape[1]
    col_count = col_points.shape[1]
    blocks = max(1, row_count * col_count // limit)
    while row_count % blocks:
        blocks = blocks - 1
    block_size = row_count // blocks
    grouped = row_points.reshape(3, blocks, block_size).transpose(1, 0, 2)

    def apply_block(row_block):
        first = row_block[0][:, None] - col_points[0][None, :]
        second = row_block[1][:, None] - col_points[1][None, :]
        third = row_block[2][:, None] - col_points[2][None, :]
        squared = first * first + second * second + third * third
        weights = lax.rsqrt(squared + softening) * kernel_scale
        return jnp.dot(
            weights, values, preferred_element_type=jnp.float32, precision=lax.Precision.HIGHEST
        )

    return lax.map(apply_block, grouped).reshape(row_count, values.shape[1])


def constants(total):
    kernel_scale = float(total) ** (-0.5)
    spacing = 0.25 * float(total) ** (-1.0 / 3.0)
    return (kernel_scale, spacing * spacing)


def squares(residual):
    return lax.psum(jnp.sum(residual * residual, axis=0), ("row", "col"))


def body(positions, radii, right_side):
    local_count = positions.shape[1]
    total = local_count * lax.axis_size("row") * lax.axis_size("col")
    kernel_scale, softening = constants(total)
    row_points = lax.all_gather(positions, "col", axis=1, tiled=True)
    col_points = lax.all_gather(positions, "row", axis=1, tiled=True)
    limit = 1 << 20
    solution = jnp.zeros_like(right_side)
    residual = right_side
    direction = right_side
    norm_now = squares(residual)
    for iteration in range(ITERS):
        col_values = lax.all_gather(direction, "row", axis=0, tiled=True)
        summed = lax.psum_scatter(
            kernel_product(row_points, col_points, col_values, kernel_scale, softening, limit),
            "col",
            scatter_dimension=0,
            tiled=True,
        )
        image_vec = direction / radii[:, None] + summed
        curvature = lax.psum(jnp.sum(direction * image_vec, axis=0), ("row", "col"))
        step_size = norm_now / curvature
        solution = solution + step_size * direction
        residual = residual - step_size * image_vec
        if iteration + 1 < ITERS:
            norm_next = squares(residual)
            direction = residual + norm_next / norm_now * direction
            norm_now = norm_next
    return (solution, residual)


def solution(mesh):
    return jax.shard_map(
        body,
        mesh=mesh,
        in_specs=(P(None, ("row", "col")), P(("row", "col")), P(("row", "col"), None)),
        out_specs=(P(("row", "col"), None), P(("row", "col"), None)),
        check_vma=False,
    )
```

profile of v0, /device:TPU:1, one launch (start us, length us, event | category | flops | bytes accessed | tf_op | source)
XLA Modules:
  0.0 550.6 jit_solution(2993443880854321543)
XLA Ops:
  7.2 0.0 all-gather.3.cloned.1.call-start
  7.2 0.7 all-gather.3.cloned.1.call-update
  7.9 0.0 reduce-scatter.3.cloned.1.call-start
  7.9 40.7 %all_gather.13 = f32[3,2048]{1,0:T(4,128)S(1)} all-gather(f32[3,128]{1,0:T(4,128)} %param.7), channel_id=1, replica_groups=mesh['row'=16,'col'=16] {'row'}, dimensions={1}, use_global_device_ids=true | all-gather | bytes 26112 | tf_op jit(solution)/shard_map/all_gather | solution.py:46
  48.7 28.0 %all_gather.12 = f32[3,2048]{1,0:T(4,128)S(1)} all-gather(f32[3,128]{1,0:T(4,128)} %param.7), channel_id=1, replica_groups=mesh['row'=16,'col'=16] {'col'}, dimensions={1}, use_global_device_ids=true | all-gather | bytes 26112 | tf_op jit(solution)/shard_map/all_gather | solution.py:45
  76.6 0.0 all-gather.3.cloned.1.call-done
  76.6 0.2 broadcast.19.clone
  76.8 25.9 %while.20 = (s32[]{:T(128)}, f32[4,512,256]{2,1,0:T(8,128)S(1)}, f32[4,3,512]{2,1,0:T(4,128)S(1)}, f32[3,2048]{1,0:T(4,128)S(1)}, f32[2048,256]{1,0:T(8,128)}, /*index=5*/s32[]{:T(128)}, s32[]{:T(128)}, s32[]{}, s32[]{}) while((s32[]{:T(128)}, f32[4,512,256]{2,1,0:T(8,128)S(1)}, f32[4,3,512]{2,1,0:T(4,128)S(1)}, f32[3,2048]{1,0:T(4,128)S(1)}, ...), condition=%wide.region_3.4_spmd, body=%wide.region_2.3_spmd.sunk | while | flops 3231711232 | bytes 2713733 | solution.py:28
  76.8 6.4 %fusion.71 = f32[4,512,256]{2,1,0:T(8,128)S(1)} fusion(f32[4,512,256]{2,1,0:T(8,128)S(1)} %get-tuple-element.194, s32[]{:T(128)} %get-tuple-element.193, f32[2048,256]{1,0:T(8,128)} %get-tuple-element.206, f32[2048]{0:T(1024)S(1)} %bitcast.63, f32[512]{0:T(512)S(1)} %bitcast.70, f32[2048]{0:T(1024)S(1)} %bitcast.64, f32[512]{0:T(512)S(1)} %bitcast.69, ...), kind=kOutput, calls=%fused_computation.21.clone.1 | convolution fusion | flops 3231711232 | bytes 2652164 | tf_op jit(solution)/shard_map/while/body/eval_jaxpr/dot_general | solution.py:24
  83.3 6.4 %fusion.71 = f32[4,512,256]{2,1,0:T(8,128)S(1)} fusion(f32[4,512,256]{2,1,0:T(8,128)S(1)} %get-tuple-element.194, s32[]{:T(128)} %get-tuple-element.193, f32[2048,256]{1,0:T(8,128)} %get-tuple-element.206, f32[2048]{0:T(1024)S(1)} %bitcast.63, f32[512]{0:T(512)S(1)} %bitcast.70, f32[2048]{0:T(1024)S(1)} %bitcast.64, f32[512]{0:T(512)S(1)} %bitcast.69, ...), kind=kOutput, calls=%fused_computation.21.clone.1 | convolution fusion | flops 3231711232 | bytes 2652164 | tf_op jit(solution)/shard_map/while/body/eval_jaxpr/dot_general | solution.py:24
  89.8 6.4 %fusion.71 = f32[4,512,256]{2,1,0:T(8,128)S(1)} fusion(f32[4,512,256]{2,1,0:T(8,128)S(1)} %get-tuple-element.194, s32[]{:T(128)} %get-tuple-element.193, f32[2048,256]{1,0:T(8,128)} %get-tuple-element.206, f32[2048]{0:T(1024)S(1)} %bitcast.63, f32[512]{0:T(512)S(1)} %bitcast.70, f32[2048]{0:T(1024)S(1)} %bitcast.64, f32[512]{0:T(512)S(1)} %bitcast.69, ...), kind=kOutput, calls=%fused_computation.21.clone.1 | convolution fusion | flops 3231711232 | bytes 2652164 | tf_op jit(solution)/shard_map/while/body/eval_jaxpr/dot_general | solution.py:24
  96.3 6.4 %fusion.71 = f32[4,512,256]{2,1,0:T(8,128)S(1)} fusion(f32[4,512,256]{2,1,0:T(8,128)S(1)} %get-tuple-element.194, s32[]{:T(128)} %get-tuple-element.193, f32[2048,256]{1,0:T(8,128)} %get-tuple-element.206, f32[2048]{0:T(1024)S(1)} %bitcast.63, f32[512]{0:T(512)S(1)} %bitcast.70, f32[2048]{0:T(1024)S(1)} %bitcast.64, f32[512]{0:T(512)S(1)} %bitcast.69, ...), kind=kOutput, calls=%fused_computation.21.clone.1 | convolution fusion | flops 3231711232 | bytes 2652164 | tf_op jit(solution)/shard_map/while/body/eval_jaxpr/dot_general | solution.py:24
  102.7 0.0 copy-start.1
  102.7 0.0 copy-start.2
  102.7 0.0 copy-start.4
  102.7 1.3 copy-done.1
  104.0 0.0 reduce-scatter.3.cloned.1.call-update
  104.1 0.0 all-gather.5.cloned.1.call-start
  104.1 58.5 %reduce-scatter.3.cloned.1.call-done = f32[128,256]{1,0:T(8,128)} async-done(((f32[2048,256]{1,0:T(8,128)}), f32[128,256]{1,0:T(8,128)}) %reduce-scatter.3.cloned.1.call-update) | async-done | bytes 131088 | tf_op jit(solution)/shard_map/reduce_scatter | solution.py:54
  162.6 0.0 copy-done.2
  162.6 0.0 copy-done.4
  162.6 1.0 multiply_reduce_fusion.2
  163.6 79.5 %all-reduce = (f32[256]{0:T(256)S(1)}, f32[256]{0:T(256)S(1)}) all-reduce(f32[256]{0:T(256)S(1)} %get-tuple-element.59, f32[256]{0:T(256)S(1)} %get-tuple-element.58), channel_id=1, replica_groups=mesh['row'=16,'col'=16] {'row','col'}, use_global_device_ids=true, to_apply=%region_1.0 | all-reduce | flops 512 | bytes 4096 | tf_op jit(solution)/shard_map/psum | solution.py:38
  243.1 1.0 multiply_reduce_fusion.1
  244.1 72.5 %psum.30 = f32[256]{0:T(256)S(1)} all-reduce(f32[256]{0:T(256)S(1)} %get-tuple-element.82), channel_id=1, replica_groups=mesh['row'=16,'col'=16] {'row','col'}, use_global_device_ids=true, to_apply=%region_8.9 | all-reduce | flops 256 | bytes 2048 | tf_op jit(solution)/shard_map/psum | solution.py:38
  316.6 0.7 multiply_add_fusion.1
  317.3 0.0 all-gather.5.cloned.1.call-update
  317.3 0.2 reduce-scatter.5.cloned.1.call-start
  317.6 55.1 %all-gather.5.cloned.1.call-done = f32[2048,256]{1,0:T(8,128)} async-done(((f32[128,256]{1,0:T(8,128)}), f32[2048,256]{1,0:T(8,128)}) %all-gather.5.cloned.1.call-update) | async-done | bytes 2097168 | tf_op jit(solution)/shard_map/all_gather | solution.py:53
  372.7 0.2 broadcast.19
  372.9 25.9 %while.21 = (s32[]{:T(128)}, f32[4,512,256]{2,1,0:T(8,128)S(1)}, f32[4,3,512]{2,1,0:T(4,128)S(1)}, f32[3,2048]{1,0:T(4,128)S(1)}, f32[2048,256]{1,0:T(8,128)}, /*index=5*/s32[]{:T(128)}, s32[]{:T(128)}, s32[]{}, s32[]{}) while((s32[]{:T(128)}, f32[4,512,256]{2,1,0:T(8,128)S(1)}, f32[4,3,512]{2,1,0:T(4,128)S(1)}, f32[3,2048]{1,0:T(4,128)S(1)}, ...), condition=%wide.region_10.11_spmd, body=%wide.region_9.10_spmd.sunk | while | flops 3231711232 | bytes 2713733 | solution.py:28
  372.9 6.4 %fusion.75 = f32[4,512,256]{2,1,0:T(8,128)S(1)} fusion(f32[4,512,256]{2,1,0:T(8,128)S(1)} %get-tuple-element.221, s32[]{:T(128)} %get-tuple-element.220, f32[2048,256]{1,0:T(8,128)} %get-tuple-element.233, f32[2048]{0:T(1024)S(1)} %bitcast.66, f32[512]{0:T(512)S(1)} %bitcast.73, f32[2048]{0:T(1024)S(1)} %bitcast.67, f32[512]{0:T(512)S(1)} %bitcast.72, ...), kind=kOutput, calls=%fused_computation.48.clone.1 | convolution fusion | flops 3231711232 | bytes 2652164 | tf_op jit(solution)/shard_map/while/body/eval_jaxpr/dot_general | solution.py:24
  379.4 6.4 %fusion.75 = f32[4,512,256]{2,1,0:T(8,128)S(1)} fusion(f32[4,512,256]{2,1,0:T(8,128)S(1)} %get-tuple-element.221, s32[]{:T(128)} %get-tuple-element.220, f32[2048,256]{1,0:T(8,128)} %get-tuple-element.233, f32[2048]{0:T(1024)S(1)} %bitcast.66, f32[512]{0:T(512)S(1)} %bitcast.73, f32[2048]{0:T(1024)S(1)} %bitcast.67, f32[512]{0:T(512)S(1)} %bitcast.72, ...), kind=kOutput, calls=%fused_computation.48.clone.1 | convolution fusion | flops 3231711232 | bytes 2652164 | tf_op jit(solution)/shard_map/while/body/eval_jaxpr/dot_general | solution.py:24
  385.9 6.4 %fusion.75 = f32[4,512,256]{2,1,0:T(8,128)S(1)} fusion(f32[4,512,256]{2,1,0:T(8,128)S(1)} %get-tuple-element.221, s32[]{:T(128)} %get-tuple-element.220, f32[2048,256]{1,0:T(8,128)} %get-tuple-element.233, f32[2048]{0:T(1024)S(1)} %bitcast.66, f32[512]{0:T(512)S(1)} %bitcast.73, f32[2048]{0:T(1024)S(1)} %bitcast.67, f32[512]{0:T(512)S(1)} %bitcast.72, ...), kind=kOutput, calls=%fused_computation.48.clone.1 | convolution fusion | flops 3231711232 | bytes 2652164 | tf_op jit(solution)/shard_map/while/body/eval_jaxpr/dot_general | solution.py:24
  392.3 6.4 %fusion.75 = f32[4,512,256]{2,1,0:T(8,128)S(1)} fusion(f32[4,512,256]{2,1,0:T(8,128)S(1)} %get-tuple-element.221, s32[]{:T(128)} %get-tuple-element.220, f32[2048,256]{1,0:T(8,128)} %get-tuple-element.233, f32[2048]{0:T(1024)S(1)} %bitcast.66, f32[512]{0:T(512)S(1)} %bitcast.73, f32[2048]{0:T(1024)S(1)} %bitcast.67, f32[512]{0:T(512)S(1)} %bitcast.72, ...), kind=kOutput, calls=%fused_computation.48.clone.1 | convolution fusion | flops 3231711232 | bytes 2652164 | tf_op jit(solution)/shard_map/while/body/eval_jaxpr/dot_general | solution.py:24
  398.7 0.0 copy-start
  398.7 0.0 copy-start.3
  398.8 1.3 copy-done
  400.1 0.0 reduce-scatter.5.cloned.1.call-update
  400.1 61.9 %reduce-scatter.5.cloned.1.call-done = f32[128,256]{1,0:T(8,128)} async-done(((f32[2048,256]{1,0:T(8,128)}), f32[128,256]{1,0:T(8,128)}) %reduce-scatter.5.cloned.1.call-update) | async-done | bytes 131088 | tf_op jit(solution)/shard_map/reduce_scatter | solution.py:54
  462.0 0.0 copy-done.3
  462.0 1.0 multiply_reduce_fusion
  463.0 79.4 %psum.31 = f32[256]{0:T(256)S(1)} all-reduce(f32[256]{0:T(256)S(1)} %multiply_reduce_fusion), channel_id=1, replica_groups=mesh['row'=16,'col'=16] {'row','col'}, use_global_device_ids=true, to_apply=%region_13.14 | all-reduce | flops 256 | bytes 2048 | tf_op jit(solution)/shard_map/psum | solution.py:61
  542.4 1.7 multiply_subtract_fusion
  (19 shorter events, 0.3 us)
Async XLA Ops:
  7.2 69.5 %all-gather.3.cloned.1.call-start = ((), (), s32[]{:S(2)}) async-start(), calls=%async_computation.2 | async-start | bytes 2228224 | tf_op jit(solution)/shard_map/all_gather | solution.py:53
  7.9 154.7 %reduce-scatter.3.cloned.1.call-start = ((), (), s32[]{:S(2)}) async-start(), calls=%async_computation.3 | async-start | bytes 2228224 | tf_op jit(solution)/shard_map/reduce_scatter | solution.py:54
  102.7 1.3 copy-start.1
  102.7 59.9 %copy-start.2 = (f32[128,256]{1,0:T(8,128)S(1)}, f32[128,256]{1,0:T(8,128)}, u32[]{:S(2)}) copy-start(f32[128,256]{1,0:T(8,128)} %param.9) | copy-start | bytes 393220
  102.7 59.9 %copy-start.4 = (f32[128]{0:T(128)S(1)}, f32[128]{0:T(128)}, u32[]{:S(2)}) copy-start(f32[128]{0:T(128)} %param.8) | copy-start | bytes 1540
  104.1 268.6 %all-gather.5.cloned.1.call-start = ((), (), s32[]{:S(2)}) async-start(), calls=%async_computation.4 | async-start | bytes 2228224 | tf_op jit(solution)/shard_map/all_gather | solution.py:53
  317.3 144.7 %reduce-scatter.5.cloned.1.call-start = ((), (), s32[]{:S(2)}) async-start(), calls=%async_computation.5 | async-start | bytes 2228224 | tf_op jit(solution)/shard_map/reduce_scatter | solution.py:54
  398.7 1.3 copy-start
  398.7 63.2 %copy-start.3 = (f32[128,256]{1,0:T(8,128)S(1)}, f32[128,256]{1,0:T(8,128)}, u32[]{:S(2)}) copy-start(f32[128,256]{1,0:T(8,128)} %multiply_add_fusion.1) | copy-start | bytes 393220
Sparse Core Ops, SparseCore 0:
  10.4 62.6 all-gather.2
  104.2 58.3 reduce-scatter.2
  317.4 55.2 all-gather.4
  400.2 61.7 reduce-scatter.4
where the time goes:
time: 551 us
  blocking collectives  300 us (54%)
  waiting for transfers between devices  176 us (32%)
  matrix products  51.2 us (9%)
  between operations  13.8 us (3%)
    psum x2, blocking collectives, squares(): return lax.psum(jnp.sum(residual * residual, axis=0), ('row', 'col'))  152 us
    reduce_scatter x2, waiting for transfers between devices, body(): lax.psum_scatter(kernel_product(row_points, col_points, col_values, kerne...  120 us
    psum x1, blocking collectives, body(): curvature = lax.psum(jnp.sum(direction * image_vec, axis=0), ('row', 'col'))  79.4 us
    all_gather x2, waiting for transfers between devices, body(): col_values = lax.all_gather(direction, 'row', axis=0, tiled=True)  55.1 us
    dot_general x8, matrix products, apply_block(): jnp.dot(weights, values, preferred_element_type=jnp.float32, precision=la...  51.2 us
    all_gather x1, blocking collectives, body(): col_points = lax.all_gather(positions, 'row', axis=1, tiled=True)  40.7 us
    all_gather x1, blocking collectives, body(): row_points = lax.all_gather(positions, 'col', axis=1, tiled=True)  28 us
  transfers between devices with their start and end apart: 4, of which 3 were waited for; matrix products, arithmetic and copies ran while one was open for 0% of the time, Pallas kernels for 0%

commit v1 on v0

--- a/solution.py
+++ b/solution.py
@@ -58,7 +58,11 @@
             tiled=True,
         )
         image_vec = direction / radii[:, None] + summed
-        curvature = lax.psum(jnp.sum(direction * image_vec, axis=0), ("row", "col"))
+
+        def update_chains(local, mesh_dim):
+            return lax.all_gather(local, axis_name=mesh_dim).sum(axis=0)
+
+        curvature = update_chains(jnp.sum(direction * image_vec, axis=0), ("row", "col"))
         step_size = norm_now / curvature
         solution = solution + step_size * direction
         residual = residual - step_size * image_vec

time: 551 us -> 1160 us (2.11)
  blocking collectives: 300 us -> 909 us
    all_gather x0 -> x2, blocking collectives: none -> 688 us  [update_chains(): return lax.all_gather(local, axis_name=mesh_dim).sum(axis=0)]
    psum x1 -> x0, blocking collectives: 79.4 us -> none  [body(): curvature = lax.psum(jnp.sum(direction * image_vec, axis=0), ('row', 'col'))]
where the time goes in v1:
time: 1160 us
  blocking collectives  909 us (78%)
  waiting for transfers between devices  176 us (15%)
  matrix products  51.2 us (4%)
  between operations  13.8 us (1%)
    all_gather x2, blocking collectives, update_chains(): return lax.all_gather(local, axis_name=mesh_dim).sum(axis=0)  688 us
    psum x2, blocking collectives, squares(): return lax.psum(jnp.sum(residual * residual, axis=0), ('row', 'col'))  152 us
    reduce_scatter x2, waiting for transfers between devices, body(): lax.psum_scatter(kernel_product(row_points, col_points, col_values, kerne...  120 us
    all_gather x2, waiting for transfers between devices, body(): col_values = lax.all_gather(direction, 'row', axis=0, tiled=True)  55.4 us
    dot_general x8, matrix products, apply_block(): jnp.dot(weights, values, preferred_element_type=jnp.float32, precision=la...  51.2 us
    all_gather x1, blocking collectives, body(): col_points = lax.all_gather(positions, 'row', axis=1, tiled=True)  40.7 us
    all_gather x1, blocking collectives, body(): row_points = lax.all_gather(positions, 'col', axis=1, tiled=True)  28 us
  transfers between devices with their start and end apart: 4, of which 3 were waited for; matrix products, arithmetic and copies ran while one was open for 0% of the time, Pallas kernels for 0%

profile of v1, /device:TPU:1, one launch (start us, length us, event | category | flops | bytes accessed | tf_op | source)
XLA Modules:
  0.0 1160.3 jit_solution(4004648520338470616)
XLA Ops:
  7.2 0.0 all-gather.7.cloned.1.call-start
  7.2 0.7 all-gather.7.cloned.1.call-update
  7.9 0.0 reduce-scatter.3.cloned.1.call-start
  7.9 40.7 %all_gather.25 = f32[3,2048]{1,0:T(4,128)S(1)} all-gather(f32[3,128]{1,0:T(4,128)} %param.7), channel_id=1, replica_groups=mesh['row'=16,'col'=16] {'row'}, dimensions={1}, use_global_device_ids=true | all-gather | bytes 26112 | tf_op jit(solution)/shard_map/all_gather | solution.py:46
  48.7 28.0 %all_gather.24 = f32[3,2048]{1,0:T(4,128)S(1)} all-gather(f32[3,128]{1,0:T(4,128)} %param.7), channel_id=1, replica_groups=mesh['row'=16,'col'=16] {'col'}, dimensions={1}, use_global_device_ids=true | all-gather | bytes 26112 | tf_op jit(solution)/shard_map/all_gather | solution.py:45
  76.6 0.0 all-gather.7.cloned.1.call-done
  76.6 0.2 broadcast.19.clone
  76.8 25.9 %while.20 = (s32[]{:T(128)}, f32[4,512,256]{2,1,0:T(8,128)S(1)}, f32[4,3,512]{2,1,0:T(4,128)S(1)}, f32[3,2048]{1,0:T(4,128)S(1)}, f32[2048,256]{1,0:T(8,128)}, /*index=5*/s32[]{:T(128)}, s32[]{:T(128)}, s32[]{}, s32[]{}) while((s32[]{:T(128)}, f32[4,512,256]{2,1,0:T(8,128)S(1)}, f32[4,3,512]{2,1,0:T(4,128)S(1)}, f32[3,2048]{1,0:T(4,128)S(1)}, ...), condition=%wide.region_3.4_spmd, body=%wide.region_2.3_spmd.sunk | while | flops 3231711232 | bytes 2713733 | solution.py:28
  76.8 6.4 fusion.71
  83.3 6.4 fusion.71
  89.8 6.4 fusion.71
  96.3 6.4 fusion.71
  102.7 0.0 copy-start
  102.7 0.0 copy-start.2
  102.7 0.0 copy-start.4
  102.7 1.3 copy-done
  104.0 0.0 reduce-scatter.3.cloned.1.call-update
  104.1 0.0 all-gather.9.cloned.1.call-start
  104.1 58.5 %reduce-scatter.3.cloned.1.call-done = f32[128,256]{1,0:T(8,128)} async-done(((f32[2048,256]{1,0:T(8,128)}), f32[128,256]{1,0:T(8,128)}) %reduce-scatter.3.cloned.1.call-update) | async-done | bytes 131088 | tf_op jit(solution)/shard_map/reduce_scatter | solution.py:54
  162.6 0.0 copy-done.2
  162.6 0.0 copy-done.4
  162.6 1.0 multiply_reduce_fusion.2
  163.6 79.5 %psum.14 = f32[256]{0:T(256)S(1)} all-reduce(f32[256]{0:T(256)S(1)} %get-tuple-element.59), channel_id=1, replica_groups=mesh['row'=16,'col'=16] {'row','col'}, use_global_device_ids=true, to_apply=%region_1.0 | all-reduce | flops 256 | bytes 2048 | tf_op jit(solution)/shard_map/psum | solution.py:38
  243.1 341.4 %all-gather.2 = f32[256,1,256]{2,1,0:T(1,128)S(1)} all-gather(f32[1,1,256]{2,1,0:T(1,128)S(1)} %bitcast.76), channel_id=2, replica_groups=mesh['row'=16,'col'=16] {'row','col'}, dimensions={0}, use_global_device_ids=true | all-gather | bytes 263168 | tf_op jit(solution)/shard_map/all_gather | solution.py:63
  584.5 0.3 reduce_sum.56
  584.8 1.0 multiply_reduce_fusion.1
  585.8 72.7 %psum.15 = f32[256]{0:T(256)S(1)} all-reduce(f32[256]{0:T(256)S(1)} %get-tuple-element.80), channel_id=1, replica_groups=mesh['row'=16,'col'=16] {'row','col'}, use_global_device_ids=true, to_apply=%region_8.9 | all-reduce | flops 256 | bytes 2048 | tf_op jit(solution)/shard_map/psum | solution.py:38
  658.5 0.7 multiply_add_fusion.1
  659.2 0.0 all-gather.9.cloned.1.call-update
  659.2 0.2 reduce-scatter.5.cloned.1.call-start
  659.5 55.4 %all-gather.9.cloned.1.call-done = f32[2048,256]{1,0:T(8,128)} async-done(((f32[128,256]{1,0:T(8,128)}), f32[2048,256]{1,0:T(8,128)}) %all-gather.9.cloned.1.call-update) | async-done | bytes 2097168 | tf_op jit(solution)/shard_map/all_gather | solution.py:53
  714.8 0.2 broadcast.19
  715.0 25.9 %while.21 = (s32[]{:T(128)}, f32[4,512,256]{2,1,0:T(8,128)S(1)}, f32[4,3,512]{2,1,0:T(4,128)S(1)}, f32[3,2048]{1,0:T(4,128)S(1)}, f32[2048,256]{1,0:T(8,128)}, /*index=5*/s32[]{:T(128)}, s32[]{:T(128)}, s32[]{}, s32[]{}) while((s32[]{:T(128)}, f32[4,512,256]{2,1,0:T(8,128)S(1)}, f32[4,3,512]{2,1,0:T(4,128)S(1)}, f32[3,2048]{1,0:T(4,128)S(1)}, ...), condition=%wide.region_10.11_spmd, body=%wide.region_9.10_spmd.sunk | while | flops 3231711232 | bytes 2713733 | solution.py:28
  715.0 6.4 fusion.75
  721.5 6.4 fusion.75
  728.0 6.4 fusion.75
  734.4 6.4 fusion.75
  740.9 0.0 copy-start.1
  740.9 0.0 copy-start.3
  740.9 1.3 copy-done.1
  742.2 0.0 reduce-scatter.5.cloned.1.call-update
  742.2 61.9 %reduce-scatter.5.cloned.1.call-done = f32[128,256]{1,0:T(8,128)} async-done(((f32[2048,256]{1,0:T(8,128)}), f32[128,256]{1,0:T(8,128)}) %reduce-scatter.5.cloned.1.call-update) | async-done | bytes 131088 | tf_op jit(solution)/shard_map/reduce_scatter | solution.py:54
  804.1 0.0 copy-done.3
  804.1 1.0 multiply_reduce_fusion
  805.1 346.6 %all-gather.3 = f32[256,1,256]{2,1,0:T(1,128)S(1)} all-gather(f32[1,1,256]{2,1,0:T(1,128)S(1)} %bitcast.77), channel_id=3, replica_groups=mesh['row'=16,'col'=16] {'row','col'}, dimensions={0}, use_global_device_ids=true | all-gather | bytes 263168 | tf_op jit(solution)/shard_map/all_gather | solution.py:63
  1151.8 0.3 reduce_sum.59
  1152.1 1.7 multiply_subtract_fusion
  (19 shorter events, 0.3 us)
Async XLA Ops:
  7.2 69.5 %all-gather.7.cloned.1.call-start = ((), (), s32[]{:S(2)}) async-start(), calls=%async_computation.2 | async-start | bytes 2228224 | tf_op jit(solution)/shard_map/all_gather | solution.py:53
  7.9 154.7 %reduce-scatter.3.cloned.1.call-start = ((), (), s32[]{:S(2)}) async-start(), calls=%async_computation.3 | async-start | bytes 2228224 | tf_op jit(solution)/shard_map/reduce_scatter | solution.py:54
  102.7 1.4 copy-start
  102.7 59.9 %copy-start.2 = (f32[128,256]{1,0:T(8,128)S(1)}, f32[128,256]{1,0:T(8,128)}, u32[]{:S(2)}) copy-start(f32[128,256]{1,0:T(8,128)} %param.9) | copy-start | bytes 393220
  102.7 59.9 %copy-start.4 = (f32[128]{0:T(128)S(1)}, f32[128]{0:T(128)}, u32[]{:S(2)}) copy-start(f32[128]{0:T(128)} %param.8) | copy-start | bytes 1540
  104.1 610.8 %all-gather.9.cloned.1.call-start = ((), (), s32[]{:S(2)}) async-start(), calls=%async_computation.4 | async-start | bytes 2228224 | tf_op jit(solution)/shard_map/all_gather | solution.py:53
  659.2 144.9 %reduce-scatter.5.cloned.1.call-start = ((), (), s32[]{:S(2)}) async-start(), calls=%async_computation.5 | async-start | bytes 2228224 | tf_op jit(solution)/shard_map/reduce_scatter | solution.py:54
  740.9 1.4 copy-start.1
  740.9 63.3 %copy-start.3 = (f32[128,256]{1,0:T(8,128)S(1)}, f32[128,256]{1,0:T(8,128)}, u32[]{:S(2)}) copy-start(f32[128,256]{1,0:T(8,128)} %multiply_add_fusion.1) | copy-start | bytes 393220
Sparse Core Ops, SparseCore 0:
  10.4 62.6 all-gather.6
  104.2 58.3 reduce-scatter.2
  659.3 55.4 all-gather.8
  742.4 61.7 reduce-scatter.4
